TPU v7x, 128 devices: a whole 4x4x4 slice. The times are simulated.
128 devices in a mesh: az: 8 (over y, z_lo), ta: 16 (over z_hi, x, core).
Axes of the slice: x: 4, y: 4, z: 4 (z_hi: 2, z_lo: 2; z = z_hi * 2 + z_lo), core: 2. Of those that a mesh axis runs over, the one named last changes fastest.
Arguments:
- initial_field: float32 [16, 2048, 8192], P(None, 'ta', 'az'), may hold values from -6 to 6
- conductivity: bfloat16 [16, 2048, 8192], P(None, 'ta', 'az'), may hold values from 0.25 to 4
- current_density: bfloat16 [16, 2048, 8192], P(None, 'ta', 'az'), may hold values from -6 to 6
- rotor_cycle: bfloat16 [2048, 8192], P('ta', 'az'), may hold values from -6 to 6
- skew_list: int32 [2048], P('ta'), may hold values from 0 to 63
Outputs:
- relaxed: float32 [16, 2048, 8192], P(None, 'ta', 'az')
Inputs may be any that keep to these rules, and one draw needn't show every extreme that they name: `skew_list`: the rotor's offset in whole panels of 128 azimuth cells at each time step.
All inputs are finite; a program needn't handle non-finite values.
Results may differ from a plain program's by a relative error of at most 0.0003.
Values may be sent and summed in bfloat16 or wider, within the bound.
A program may use at most 192 MiB of HBM per device.

v0:
```python
import jax
import jax.numpy as jnp
from jax import lax
from jax.experimental import pallas as pl
from jax.experimental.pallas import tpu as pltpu
from jax.sharding import PartitionSpec as P

F32, BF16 = jnp.float32, jnp.bfloat16
MESH = pl.DeviceIdType.MESH
NAZ, NTA = 8, 16
NK, NJ, ROWS, T0 = 8, 9, 152, 12
PITCH = NJ * ROWS
SIXTY = 1.0 / 48.0
LIMIT = 29700 * 1024
LIMIT2 = 29700 * 1024
RED_ROWS = ((3, 4, 5, 6, 7), (0, 1, 2, 3, 4))
BLACK_ROWS = ((4, 5, 6, 7), (0, 1, 2, 3))
COEF_ROWS = (((5, 0), (6, 0), (7, 0), (6, 1), (7, 1)), ((0, 0), (1, 0), (2, 0), (0, 1), (1, 1)))


def row(kk, j, rho):
    return kk * PITCH + j * ROWS + rho


def exchange(u_hbm, s_hbm, c_hbm, rot_hbm, sk, r_a, b_a, sg, jg,
             us, ss, cs, eu, es, ec, er, su, ts, tc, hu, hs, hc, ku, ks, kc, pu, ps, pc, pd, qu, qs, qc, qd,
             w0, w1, v, cyc, cych,
             in_sem, edge_sem, col_sem, own_sem, p1s, p1r, p3s, p3r, azs, azr, tas, tar, dis, dir_, cys, cyr):
    az, ta = lax.axis_index("az"), lax.axis_index("ta")
    up, down = lax.rem(ta + NTA - 1, NTA), lax.rem(ta + 1, NTA)
    left_az, right_az = lax.rem(az + NAZ - 1, NAZ), lax.rem(az + 1, NAZ)
    others = [lax.rem(az + o, NAZ) for o in range(1, NAZ)]
    diagonals = [(side, other, t, a) for side, t in ((0, down), (1, up)) for other, a in ((0, right_az), (1, left_az))]

    rowi = lax.broadcasted_iota(jnp.int32, (8, 128), 0)
    lane = lax.broadcasted_iota(jnp.int32, (8, 128), 1)
    odd = ((rowi + lane) & 1) == 1
    lane16 = lax.broadcasted_iota(jnp.int32, (16, 128), 1)
    row16 = lax.broadcasted_iota(jnp.int32, (16, 128), 0)
    odd16 = ((lane16 + row16) & 1) == 1
    low16 = lane16 < 64

    def remote(src, dst, ssem, rsem, dev):
        return pltpu.make_async_remote_copy(src_ref=src, dst_ref=dst, send_sem=ssem, recv_sem=rsem,
                                            device_id=dev, device_id_type=MESH)

    def in_copies(k, slot):
        pair = pl.ds(2 * k, 2)
        return [pltpu.make_async_copy(h.at[pair], dst.at[slot], in_sem.at[i, slot])
                for i, (h, dst) in enumerate(((u_hbm, us), (s_hbm, ss), (c_hbm, cs)))]

    edges = [pltpu.make_async_copy(h.at[:, pl.ds(t, 8), :], e.at[side], edge_sem.at[q, side])
             for q, (h, e) in enumerate(((u_hbm, eu), (s_hbm, es), (c_hbm, ec))) for side, t in ((0, 120), (1, 0))]
    cols = [pltpu.make_async_copy(h.at[:, :, pl.ds(n, 128)], e.at[side], col_sem.at[q, side])
            for q, (h, e) in enumerate(((u_hbm, ku), (s_hbm, ks), (c_hbm, kc))) for side, n in ((0, 0), (1, 896))]

    barrier = pltpu.get_barrier_semaphore()
    for d in others:
        pl.semaphore_signal(barrier, inc=1, device_id={"az": d}, device_id_type=MESH)
    for t in (up, down):
        for a in range(NAZ):
            pl.semaphore_signal(barrier, inc=1, device_id={"ta": t, "az": a}, device_id_type=MESH)
    for c in edges: c.start()
    for c in cols: c.start()
    own = pltpu.make_async_copy(rot_hbm.at[pl.ds(16 * az, 16), :], w0.at[:, pl.ds(1024 * az, 1024)], own_sem.at[0])
    own.start()
    for c in in_copies(NK - 1, 0): c.start()
    for c in in_copies(NK - 2, 1): c.start()
    pl.semaphore_wait(barrier, 3 * NAZ - 1)
    first_hop = [remote(rot_hbm.at[pl.ds(16 * d, 16), :], w0.at[:, pl.ds(1024 * az, 1024)], p1s.at[o], p1r.at[o], {"az": d})
                 for o, d in enumerate(others)]
    for c in first_hop: c.start()

    for c in edges: c.wait()
    for side in range(2):
        for q, e in enumerate((eu, es, ec)):
            for j in range(8):
                ln = slice(128 * j, 128 * j + 128)
                base = ((q * 2 + side) * 8 + j) * 128
                for k in range(NK):
                    even, odd_layer = e[side, 2 * k, :, ln].astype(F32), e[side, 2 * k + 1, :, ln].astype(F32)
                    er[base + 8 * k:base + 8 * k + 8, :] = jnp.where(odd, odd_layer, even)
                    er[base + 64 + 8 * k:base + 72 + 8 * k, :] = jnp.where(odd, even, odd_layer)
                if q == 0:
                    for i, t in enumerate(RED_ROWS[side]):
                        su[side, i, :, ln] = er[pl.ds(base + t, NK, stride=8), :]
                    for i, t in enumerate(BLACK_ROWS[side]):
                        su[side, 5 + i, :, ln] = er[pl.ds(base + 64 + t, NK, stride=8), :]
                else:
                    for i, (t, colour) in enumerate(COEF_ROWS[side]):
                        (ts if q == 1 else tc)[side, i, :, ln] = er[pl.ds(base + 64 * colour + t, NK, stride=8), :].astype(BF16)
    time_hop = [remote(a.at[side], b.at[side], tas.at[side, q], tar.at[side, q], {"ta": d})
                for side, d in ((0, down), (1, up)) for q, (a, b) in enumerate(((su, hu), (ts, hs), (tc, hc)))]
    for c in time_hop: c.start()

    for c in cols: c.wait()

    def columns(i, _):
        rows = pl.ds(pl.multiple_of(16 * i, 16), 16)
        for src, dst in ((ku, pu), (ks, ps), (kc, pc)):
            acc = jnp.zeros((16, 128), F32)
            for k in range(NK):
                even = jnp.where(low16, src[0, 2 * k, rows, :].astype(F32), src[1, 2 * k, rows, :].astype(F32))
                odd_l = jnp.where(low16, src[0, 2 * k + 1, rows, :].astype(F32), src[1, 2 * k + 1, rows, :].astype(F32))
                red, black = jnp.where(odd16, odd_l, even), jnp.where(odd16, even, odd_l)
                for a, x in ((k, red), (k + 8, black)):
                    acc = jnp.where((lane16 >> 3) == a, pltpu.roll(x, (8 * a + 4) % 128, 1), acc)
            dst[rows, :] = acc.astype(dst.dtype)
        return 0
    lax.fori_loop(0, 8, columns, 0)
    for q, src in enumerate((pu, ps, pc)):
        pd[0, q] = src[112:128, :].astype(F32)[8:]
        pd[1, q] = src[0:16, :].astype(F32)[:8]
    az_hop = [remote(a, b.at[side], azs.at[side, q], azr.at[side, q], {"az": d})
              for side, d in ((0, right_az), (1, left_az)) for q, (a, b) in enumerate(((pu, qu), (ps, qs), (pc, qc)))]
    diag_hop = [remote(pd.at[side], qd.at[side, other], dis.at[side, other], dir_.at[side, other], {"ta": t, "az": a})
                for side, other, t, a in diagonals]
    for c in az_hop + diag_hop: c.start()

    def pack(s, _):
        k = NK - 1 - s
        slot = lax.rem(s, 2)
        for c in in_copies(k, slot): c.wait()
        st, c0, c1 = (k + 1) * PITCH, k * PITCH, (k + NK) * PITCH
        for i in range(8):
            rows = slice(16 * i, 16 * i + 16)
            for j in range(8):
                ln = slice(128 * j, 128 * j + 128)
                e16, o16 = ss[slot, 0, rows, ln].astype(F32) * SIXTY, ss[slot, 1, rows, ln].astype(F32) * SIXTY
                f16, p16 = cs[slot, 0, rows, ln].astype(F32), cs[slot, 1, rows, ln].astype(F32)
                for h in range(2):
                    part, r8 = slice(8 * h, 8 * h + 8), slice(16 * i + 8 * h, 16 * i + 8 * h + 8)
                    at = j * ROWS + T0 + 16 * i + 8 * h
                    for e, o, ra, rb, pa, pb in ((us[slot, 0, r8, ln], us[slot, 1, r8, ln], r_a, b_a, st, st),
                                                 (e16[part], o16[part], sg, sg, c0, c1), (f16[part], p16[part], jg, jg, c0, c1)):
                        ra[pl.ds(pa + at, 8), :] = jnp.where(odd, o, e)
                        rb[pl.ds(pb + at, 8), :] = jnp.where(odd, e, o)

        @pl.when(s + 2 < NK)
        def _():
            for c in in_copies(k - 2, slot): c.start()
        return 0

    own.wait()
    for c in first_hop: c.wait_recv()
    amount = sk[pl.ds(pl.multiple_of(16 * az, 16), 16), :]
    src, dst = w0, w1
    for b in range(6):
        bit = ((amount >> b) & 1) == 1
        for p in range(64):
            f = (p - (1 << b)) % 64
            dst[:, 128 * p:128 * p + 128] = jnp.where(bit, src[:, 128 * f:128 * f + 128], src[:, 128 * p:128 * p + 128])
        src, dst = dst, src
    for d in range(NAZ):
        for jj in range(8):
            v[d, jj] = w0[:, 1024 * d + 128 * jj:1024 * d + 128 * jj + 128]
        after, before = (8 * d + 8) % 64, (8 * d - 1) % 64
        v[d, 8] = jnp.where(low16, w0[:, 128 * after:128 * after + 128], w0[:, 128 * before:128 * before + 128])
    block = pl.ds(16 * az, 16)
    mine = pltpu.make_async_copy(v.at[az], cyc.at[:, block, :], own_sem.at[1])
    mine.start()
    second_hop = [remote(v.at[d], cyc.at[:, block, :], p3s.at[o], p3r.at[o], {"az": d}) for o, d in enumerate(others)]
    for c in second_hop: c.start()
    beyond = [[remote(v.at[d], cych.at[side], cys.at[d], cyr.at[side], {"ta": t, "az": d}) for d in range(NAZ)]
              for side, t in ((0, down), (1, up))]

    @pl.when(az == NAZ - 1)
    def _():
        for c in beyond[0]: c.start()

    @pl.when(az == 0)
    def _():
        for c in beyond[1]: c.start()

    lax.fori_loop(0, NK, pack, 0)

    zero = jnp.zeros((8, 128), F32)
    for j in range(NJ):
        for i in range(ROWS // 8):
            for ref in (r_a, b_a):
                ref[pl.ds(row(NK + 1, j, 8 * i), 8), :] = zero

    for c in az_hop: c.wait_recv()
    for c in diag_hop: c.wait_recv()
    mine_lane = (lane & 7) < 4
    mine16 = (lane16 & 7) < 4

    def place(q, x, rho):
        if q == 1:
            x = x * SIXTY
        for a in range(16):
            y = pltpu.roll(x, (124 - 8 * a) % 128, 1)
            if q == 0:
                (r_a if a < 8 else b_a)[pl.ds(row(a % 8 + 1, NJ - 1, rho), 8), :] = y
            else:
                (sg if q == 1 else jg)[pl.ds(a * PITCH + (NJ - 1) * ROWS + rho, 8), :] = y

    for q, b in enumerate((qu, qs, qc)):
        for side, rho in ((0, T0 - 8), (1, T0 + 128)):
            place(q, jnp.where(mine_lane, qd[side, 0, q], qd[side, 1, q]), rho)
        for i in range(8):
            x = jnp.where(mine16, b[0, 16 * i:16 * i + 16, :].astype(F32), b[1, 16 * i:16 * i + 16, :].astype(F32))
            for h in range(2):
                place(q, x[8 * h:8 * h + 8], T0 + 16 * i + 8 * h)

    mine.wait()
    for c in second_hop: c.wait_recv()
    for side in range(2): beyond[side][0].wait_recv()
    for j in range(NJ):
        for i in range(8):
            x = cyc[j, 16 * i:16 * i + 16, :].astype(F32)
            for ref in (r_a, b_a):
                ref[pl.ds(row(0, j, T0 + 16 * i), 16), :] = x
        top, bottom = cych[0, j].astype(F32)[8:], cych[1, j].astype(F32)[:8]
        for ref in (r_a, b_a):
            ref[pl.ds(row(0, j, T0 - 8), 8), :] = top
            ref[pl.ds(row(0, j, T0 + 128), 8), :] = bottom

    for c in time_hop: c.wait_recv()

    def spread(ref, base, j, t, tile):
        ref[pl.ds(base + j * ROWS + T0 + t, NK, stride=PITCH), :] = tile

    for j in range(8):
        ln = slice(128 * j, 128 * j + 128)
        for side in range(2):
            shift = -8 if side == 0 else 128
            for i, t in enumerate(RED_ROWS[side]):
                spread(r_a, PITCH, j, t + shift, hu[side, i, :, ln])
            for i, t in enumerate(BLACK_ROWS[side]):
                spread(b_a, PITCH, j, t + shift, hu[side, 5 + i, :, ln])
            for i, (t, colour) in enumerate(COEF_ROWS[side]):
                spread(sg, colour * NK * PITCH, j, t + shift, hs[side, i, :, ln].astype(F32) * SIXTY)
                spread(jg, colour * NK * PITCH, j, t + shift, hc[side, i, :, ln].astype(F32))

    for c in first_hop + second_hop + time_hop + az_hop + diag_hop: c.wait_send()

    @pl.when(az == NAZ - 1)
    def _():
        for c in beyond[0]: c.wait_send()

    @pl.when(az == 0)
    def _():
        for c in beyond[1]: c.wait_send()


def relax(r_0, b_0, sg, jg, out_hbm, r_1, b_1, r_2, outs, out_sem):
    rowi = lax.broadcasted_iota(jnp.int32, (8, 128), 0)
    lane = lax.broadcasted_iota(jnp.int32, (8, 128), 1)
    odd = ((rowi + lane) & 1) == 1
    first, last = lane == 0, lane == 127

    def out_copy(k, slot):
        return pltpu.make_async_copy(outs.at[slot], out_hbm.at[pl.ds(2 * k, 2)], out_sem.at[slot])

    zero = jnp.zeros((8, 128), F32)
    for j in range(NJ):
        for i in range(ROWS // 8):
            x = r_0[pl.ds(row(0, j, 8 * i), 8), :]
            for ref in (r_1, b_1, r_2):
                ref[pl.ds(row(NK + 1, j, 8 * i), 8), :] = zero
                ref[pl.ds(row(0, j, 8 * i), 8), :] = x

    def half(k, colour, src, own, rho, nj, emit):
        st = (k + 1) * PITCH
        co = (k + colour * NK) * PITCH
        cen = [src[pl.ds(st + j * ROWS + rho, 8), :] for j in range(NJ)]
        rl = [pltpu.roll(x, 1, 1) for x in cen]
        rr = [pltpu.roll(x, 127, 1) for x in cen]
        for j in range(nj):
            off = j * ROWS + rho
            left = jnp.where(first, rl[(j - 1) % NJ], rl[j])
            right = jnp.where(last, rr[(j + 1) % NJ], rr[j])
            lo, hi = src[pl.ds(st - PITCH + off, 8), :], src[pl.ds(st + PITCH + off, 8), :]
            rad = jnp.where(odd, hi, lo) if colour == 0 else jnp.where(odd, lo, hi)
            d1 = src[pl.ds(st + off + 1, 8), :] - src[pl.ds(st + off - 1, 8), :]
            d2 = own[pl.ds(st + off + 2, 8), :] - own[pl.ds(st + off - 2, 8), :]
            acc = ((jg[pl.ds(co + off, 8), :] + rad) + cen[j]) + (left + right)
            emit(j, rho, acc * 0.25 - sg[pl.ds(co + off, 8), :] * (d1 * 8.0 - d2))

    def unit(k, colour, src, own, dst):
        st = (k + 1) * PITCH

        def emit(j, rho, val):
            dst[pl.ds(st + j * ROWS + rho, 8), :] = val
        for i in range(17):
            half(k, colour, src, own, 8 + 8 * i, NJ, emit)

    def final(k, slot):
        st = (k + 1) * PITCH

        def emit(j, rho, val):
            red = r_2[pl.ds(st + j * ROWS + rho, 8), :]
            t = rho - T0
            outs[slot, 0, t:t + 8, 128 * j:128 * j + 128] = jnp.where(odd, val, red)
            outs[slot, 1, t:t + 8, 128 * j:128 * j + 128] = jnp.where(odd, red, val)
        for i in range(16):
            half(k, 1, r_2, b_1, T0 + 8 * i, 8, emit)

    def step(s, _):
        @pl.when(s < NK)
        def _():
            unit(NK - 1 - s, 0, b_0, r_0, r_1)

        @pl.when((s >= 1) & (s < NK + 1))
        def _():
            unit(NK - s, 1, r_1, b_0, b_1)

        @pl.when((s >= 2) & (s < NK + 2))
        def _():
            unit(NK + 1 - s, 0, b_1, r_1, r_2)

        @pl.when(s >= 3)
        def _():
            k = NK + 2 - s
            slot = lax.rem(s, 2)

            @pl.when(s >= 5)
            def _():
                out_copy(k + 2, slot).wait()
            final(k, slot)
            out_copy(k, slot).start()
        return 0
    lax.fori_loop(0, NK + 3, step, 0)
    out_copy(1, 1).wait()
    out_copy(0, 0).wait()


def local(u, s, c, rot, skew):
    sk = jnp.broadcast_to(skew[:, None], (128, 128))
    anys = pl.BlockSpec(memory_space=pl.ANY)
    vm = pl.BlockSpec(memory_space=pltpu.VMEM)
    D, V = pltpu.SemaphoreType.DMA, pltpu.VMEM
    state = V(((NK + 2) * PITCH, 128), F32)
    coef = V((2 * NK * PITCH, 128), F32)
    packed = pl.pallas_call(
        exchange,
        out_shape=(state, state, coef, coef),
        in_specs=[anys] * 4 + [vm],
        out_specs=(vm,) * 4,
        scratch_shapes=[V((2, 2, 128, 1024), F32), V((2, 2, 128, 1024), BF16), V((2, 2, 128, 1024), BF16),
                        V((2, 16, 8, 1024), F32), V((2, 16, 8, 1024), BF16), V((2, 16, 8, 1024), BF16),
                        V((3 * 2 * 8 * 128, 128), F32),
                        V((2, 9, 8, 1024), F32), V((2, 5, 8, 1024), BF16), V((2, 5, 8, 1024), BF16),
                        V((2, 9, 8, 1024), F32), V((2, 5, 8, 1024), BF16), V((2, 5, 8, 1024), BF16),
                        V((2, 16, 128, 128), F32), V((2, 16, 128, 128), BF16), V((2, 16, 128, 128), BF16),
                        V((128, 128), F32), V((128, 128), BF16), V((128, 128), BF16), V((2, 3, 8, 128), F32),
                        V((2, 128, 128), F32), V((2, 128, 128), BF16), V((2, 128, 128), BF16), V((2, 2, 3, 8, 128), F32),
                        V((16, 8192), BF16), V((16, 8192), BF16), V((8, 9, 16, 128), BF16),
                        V((9, 128, 128), BF16), V((2, 9, 16, 128), BF16),
                        D((3, 2)), D((3, 2)), D((3, 2)), D((2,)), D((7,)), D((7,)), D((7,)), D((7,)), D((2, 3)), D((2, 3)),
                        D((2, 3)), D((2, 3)), D((2, 2)), D((2, 2)), D((8,)), D((2,))],
        compiler_params=pltpu.CompilerParams(collective_id=0, has_side_effects=True, vmem_limit_bytes=LIMIT),
        name="exchange",
    )(u, s, c, rot, sk)
    return pl.pallas_call(
        relax,
        out_shape=jax.ShapeDtypeStruct((16, 128, 1024), F32),
        in_specs=[vm] * 4,
        out_specs=anys,
        scratch_shapes=[state, state, state, V((2, 2, 128, 1024), F32), D((2,))],
        compiler_params=pltpu.CompilerParams(vmem_limit_bytes=LIMIT2),
        name="relax",
    )(*[pltpu.with_memory_space_constraint(x, pltpu.VMEM) for x in packed])


def solution(mesh):
    placed = (P(None, "ta", "az"), P(None, "ta", "az"), P(None, "ta", "az"), P("ta", "az"), P("ta"))
    return jax.shard_map(
        local, mesh=mesh, in_specs=placed, out_specs=P(None, "ta", "az"), check_vma=False
    )
```

profile of v0, /device:TPU:0, one launch (start us, length us, event | category | flops | bytes accessed | tf_op | source)
XLA Modules:
  0.0 51.1 jit_solution(4131766953648018935)
XLA Ops:
  0.0 1.4 %broadcast_in_dim.2.sk = s32[128,128]{1,0:T(8,128)} broadcast(s32[128]{0:T(128)} %param.9), dimensions={0} | broadcast | bytes 66048 | tf_op jit(solution)/shard_map/broadcast_in_dim | solution.py:330
  1.4 32.1 %exchange.1 = (f32[13680,128]{1,0:T(8,128)S(1)}, f32[13680,128]{1,0:T(8,128)S(1)}, f32[21888,128]{1,0:T(8,128)S(1)}, f32[21888,128]{1,0:T(8,128)S(1)}) custom-call(f32[16,128,1024]{2,1,0:T(8,128)} %u_hbm.1, bf16[16,128,1024]{2,1,0:T(8,128)(2,1)} %s_hbm.1, bf16[16,128,1024]{2,1,0:T(8,128)(2,1)} %c_hbm.1, bf16[128,1024]{1,0:T(8,128)(2,1)} %rot_hbm.1, ...), custom_call_target="tpu_custom_call" | custom-call | tf_op jit(solution)/shard_map/exchange/pallas_call | solution.py:336
  33.5 17.6 %relax.1 = f32[16,128,1024]{2,1,0:T(8,128)} custom-call(f32[13680,128]{1,0:T(8,128)S(1)} %get-tuple-element.9.r_0, f32[13680,128]{1,0:T(8,128)S(1)} %get-tuple-element.10.b_0, f32[21888,128]{1,0:T(8,128)S(1)} %get-tuple-element.11.sg, f32[21888,128]{1,0:T(8,128)S(1)} %get-tuple-element.12.jg), custom_call_target="tpu_custom_call" | custom-call | tf_op jit(solution)/shard_map/relax/pallas_call | solution.py:356
where the time goes:
time: 51.3 us; the launch traced here: 51.1 us
  Pallas kernels  49.7 us (97%)
  local copies, waits for them, and re-layouts  1.37 us (3%)
    pallas_call x1, Pallas kernels, local(): pl.pallas_call(exchange, out_shape=(state, state, coef, coef), in_specs=[...  32.1 us
    pallas_call x1, Pallas kernels, local(): pl.pallas_call(relax, out_shape=jax.ShapeDtypeStruct((16, 128, 1024), F32...  17.6 us
    broadcast_in_dim x1, local copies, waits for them, and re-layouts, local(): sk = jnp.broadcast_to(skew[:, None], (128, 128))  1.37 us

commit v1 on v0

--- a/solution.py
+++ b/solution.py
@@ -11,10 +11,9 @@
 NK, NJ, ROWS, T0 = 8, 9, 152, 12
 PITCH = NJ * ROWS
 SIXTY = 1.0 / 48.0
-LIMIT = 29700 * 1024
-LIMIT2 = 29700 * 1024
+LIMIT = 16100 * 1024
 RED_ROWS = ((3, 4, 5, 6, 7), (0, 1, 2, 3, 4))
-BLACK_ROWS = ((4, 5, 6, 7), (0, 1, 2, 3))
+BLACK_ROWS = ((7, 6, 5, 4), (0, 1, 2, 3))
 COEF_ROWS = (((5, 0), (6, 0), (7, 0), (6, 1), (7, 1)), ((0, 0), (1, 0), (2, 0), (0, 1), (1, 1)))
 
 
@@ -22,8 +21,46 @@
     return kk * PITCH + j * ROWS + rho
 
 
-def exchange(u_hbm, s_hbm, c_hbm, rot_hbm, sk, r_a, b_a, sg, jg,
-             us, ss, cs, eu, es, ec, er, su, ts, tc, hu, hs, hc, ku, ks, kc, pu, ps, pc, pd, qu, qs, qc, qd,
+def sweep(fn, top, bottom):
+    def one(i, _):
+        fn(top - i)
+        return 0
+    lax.fori_loop(0, top - bottom + 1, one, 0)
+
+
+def half(k, colour, src, own, sg, jg, rho, nj, emit):
+    rowi = lax.broadcasted_iota(jnp.int32, (8, 128), 0)
+    lane = lax.broadcasted_iota(jnp.int32, (8, 128), 1)
+    odd = ((rowi + lane) & 1) == 1
+    first, last = lane == 0, lane == 127
+    st = (k + 1) * PITCH
+    co = (k + colour * NK) * PITCH
+    cen = [src[pl.ds(st + j * ROWS + rho, 8), :] for j in range(NJ)]
+    rl = [pltpu.roll(x, 1, 1) for x in cen]
+    rr = [pltpu.roll(x, 127, 1) for x in cen]
+    for j in range(nj):
+        off = j * ROWS + rho
+        left = jnp.where(first, rl[(j - 1) % NJ], rl[j])
+        right = jnp.where(last, rr[(j + 1) % NJ], rr[j])
+        lo, hi = src[pl.ds(st - PITCH + off, 8), :], src[pl.ds(st + PITCH + off, 8), :]
+        rad = jnp.where(odd, hi, lo) if colour == 0 else jnp.where(odd, lo, hi)
+        d1 = src[pl.ds(st + off + 1, 8), :] - src[pl.ds(st + off - 1, 8), :]
+        d2 = own[pl.ds(st + off + 2, 8), :] - own[pl.ds(st + off - 2, 8), :]
+        acc = ((jg[pl.ds(co + off, 8), :] + rad) + cen[j]) + (left + right)
+        emit(j, rho, acc * 0.25 - sg[pl.ds(co + off, 8), :] * (d1 * 8.0 - d2))
+
+
+def update(k, colour, src, own, dst, sg, jg, tiles):
+    st = (k + 1) * PITCH
+
+    def emit(j, rho, val):
+        dst[pl.ds(st + j * ROWS + rho, 8), :] = val
+    for i in tiles:
+        half(k, colour, src, own, sg, jg, 8 + 8 * i, NJ, emit)
+
+
+def exchange(u_hbm, s_hbm, c_hbm, rot_hbm, sk, r_a, b_a, sg, jg, r_b, b_b,
+             us, ss, cs, eu, es, ec, er, su, tb, hu, hb, ku, ks, kc, pu, ps, pc, pd, fu, fs, fc, qu, qs, qc, qd,
              w0, w1, v, cyc, cych,
              in_sem, edge_sem, col_sem, own_sem, p1s, p1r, p3s, p3r, azs, azr, tas, tar, dis, dir_, cys, cyr):
     az, ta = lax.axis_index("az"), lax.axis_index("ta")
@@ -76,21 +113,25 @@
         for q, e in enumerate((eu, es, ec)):
             for j in range(8):
                 ln = slice(128 * j, 128 * j + 128)
-                base = ((q * 2 + side) * 8 + j) * 128
+                base = (side * 8 + j) * 128
                 for k in range(NK):
                     even, odd_layer = e[side, 2 * k, :, ln].astype(F32), e[side, 2 * k + 1, :, ln].astype(F32)
                     er[base + 8 * k:base + 8 * k + 8, :] = jnp.where(odd, odd_layer, even)
                     er[base + 64 + 8 * k:base + 72 + 8 * k, :] = jnp.where(odd, even, odd_layer)
                 if q == 0:
                     for i, t in enumerate(RED_ROWS[side]):
-                        su[side, i, :, ln] = er[pl.ds(base + t, NK, stride=8), :]
+                        tb[side, i, :, ln] = er[pl.ds(base + t, NK, stride=8), :].astype(BF16)
                     for i, t in enumerate(BLACK_ROWS[side]):
-                        su[side, 5 + i, :, ln] = er[pl.ds(base + 64 + t, NK, stride=8), :]
+                        tile = er[pl.ds(base + 64 + t, NK, stride=8), :]
+                        if i < 2:
+                            su[side, i, :, ln] = tile
+                        else:
+                            tb[side, 3 + i, :, ln] = tile.astype(BF16)
                 else:
                     for i, (t, colour) in enumerate(COEF_ROWS[side]):
-                        (ts if q == 1 else tc)[side, i, :, ln] = er[pl.ds(base + 64 * colour + t, NK, stride=8), :].astype(BF16)
+                        tb[side, 2 + 5 * q + i, :, ln] = er[pl.ds(base + 64 * colour + t, NK, stride=8), :].astype(BF16)
     time_hop = [remote(a.at[side], b.at[side], tas.at[side, q], tar.at[side, q], {"ta": d})
-                for side, d in ((0, down), (1, up)) for q, (a, b) in enumerate(((su, hu), (ts, hs), (tc, hc)))]
+                for side, d in ((0, down), (1, up)) for q, (a, b) in enumerate(((su, hu), (tb, hb)))]
     for c in time_hop: c.start()
 
     for c in cols: c.wait()
@@ -111,8 +152,14 @@
     for q, src in enumerate((pu, ps, pc)):
         pd[0, q] = src[112:128, :].astype(F32)[8:]
         pd[1, q] = src[0:16, :].astype(F32)[:8]
-    az_hop = [remote(a, b.at[side], azs.at[side, q], azr.at[side, q], {"az": d})
-              for side, d in ((0, right_az), (1, left_az)) for q, (a, b) in enumerate(((pu, qu), (ps, qs), (pc, qc)))]
+    mine16 = (lane16 & 7) < 4
+    for src, dst in ((pu, fu), (ps, fs), (pc, fc)):
+        for i in range(4):
+            early, late = src[16 * i:16 * i + 16, :].astype(F32), src[64 + 16 * i:80 + 16 * i, :].astype(F32)
+            dst[0, 16 * i:16 * i + 16, :] = jnp.where(mine16, early, pltpu.roll(late, 4, 1)).astype(dst.dtype)
+            dst[1, 16 * i:16 * i + 16, :] = jnp.where(mine16, pltpu.roll(early, 124, 1), late).astype(dst.dtype)
+    az_hop = [remote(a.at[side], b.at[side], azs.at[side, q], azr.at[side, q], {"az": d})
+              for side, d in ((0, right_az), (1, left_az)) for q, (a, b) in enumerate(((fu, qu), (fs, qs), (fc, qc)))]
     diag_hop = [remote(pd.at[side], qd.at[side, other], dis.at[side, other], dir_.at[side, other], {"ta": t, "az": a})
                 for side, other, t, a in diagonals]
     for c in az_hop + diag_hop: c.start()
@@ -177,13 +224,12 @@
     zero = jnp.zeros((8, 128), F32)
     for j in range(NJ):
         for i in range(ROWS // 8):
-            for ref in (r_a, b_a):
+            for ref in (b_a, r_b, b_b):
                 ref[pl.ds(row(NK + 1, j, 8 * i), 8), :] = zero
 
     for c in az_hop: c.wait_recv()
     for c in diag_hop: c.wait_recv()
     mine_lane = (lane & 7) < 4
-    mine16 = (lane16 & 7) < 4
 
     def place(q, x, rho):
         if q == 1:
@@ -198,10 +244,16 @@
     for q, b in enumerate((qu, qs, qc)):
         for side, rho in ((0, T0 - 8), (1, T0 + 128)):
             place(q, jnp.where(mine_lane, qd[side, 0, q], qd[side, 1, q]), rho)
-        for i in range(8):
-            x = jnp.where(mine16, b[0, 16 * i:16 * i + 16, :].astype(F32), b[1, 16 * i:16 * i + 16, :].astype(F32))
+        for i in range(4):
+            lt, rt = b[0, 16 * i:16 * i + 16, :].astype(F32), b[1, 16 * i:16 * i + 16, :].astype(F32)
+            early = jnp.where(mine16, lt, pltpu.roll(rt, 4, 1))
+            late = jnp.where(mine16, pltpu.roll(lt, 124, 1), rt)
             for h in range(2):
-                place(q, x[8 * h:8 * h + 8], T0 + 16 * i + 8 * h)
+                place(q, early[8 * h:8 * h + 8], T0 + 16 * i + 8 * h)
+                place(q, late[8 * h:8 * h + 8], T0 + 64 + 16 * i + 8 * h)
+
+    sweep(lambda k: update(k, 0, b_a, r_a, r_b, sg, jg, range(1, 16)), 7, 1)
+    sweep(lambda k: update(k, 1, r_b, b_a, b_b, sg, jg, range(2, 15)), 7, 2)
 
     mine.wait()
     for c in second_hop: c.wait_recv()
@@ -209,10 +261,10 @@
     for j in range(NJ):
         for i in range(8):
             x = cyc[j, 16 * i:16 * i + 16, :].astype(F32)
-            for ref in (r_a, b_a):
+            for ref in (b_a, r_b, b_b):
                 ref[pl.ds(row(0, j, T0 + 16 * i), 16), :] = x
         top, bottom = cych[0, j].astype(F32)[8:], cych[1, j].astype(F32)[:8]
-        for ref in (r_a, b_a):
+        for ref in (b_a, r_b, b_b):
             ref[pl.ds(row(0, j, T0 - 8), 8), :] = top
             ref[pl.ds(row(0, j, T0 + 128), 8), :] = bottom
 
@@ -226,12 +278,12 @@
         for side in range(2):
             shift = -8 if side == 0 else 128
             for i, t in enumerate(RED_ROWS[side]):
-                spread(r_a, PITCH, j, t + shift, hu[side, i, :, ln])
+                spread(r_a, PITCH, j, t + shift, hb[side, i, :, ln].astype(F32))
             for i, t in enumerate(BLACK_ROWS[side]):
-                spread(b_a, PITCH, j, t + shift, hu[side, 5 + i, :, ln])
+                spread(b_a, PITCH, j, t + shift, hu[side, i, :, ln] if i < 2 else hb[side, 3 + i, :, ln].astype(F32))
             for i, (t, colour) in enumerate(COEF_ROWS[side]):
-                spread(sg, colour * NK * PITCH, j, t + shift, hs[side, i, :, ln].astype(F32) * SIXTY)
-                spread(jg, colour * NK * PITCH, j, t + shift, hc[side, i, :, ln].astype(F32))
+                spread(sg, colour * NK * PITCH, j, t + shift, hb[side, 7 + i, :, ln].astype(F32) * SIXTY)
+                spread(jg, colour * NK * PITCH, j, t + shift, hb[side, 12 + i, :, ln].astype(F32))
 
     for c in first_hop + second_hop + time_hop + az_hop + diag_hop: c.wait_send()
 
@@ -244,11 +296,10 @@
         for c in beyond[1]: c.wait_send()
 
 
-def relax(r_0, b_0, sg, jg, out_hbm, r_1, b_1, r_2, outs, out_sem):
+def relax(r_0, b_0, sg, jg, _r, _b, out_hbm, r_1, b_1, r_2, outs, out_sem):
     rowi = lax.broadcasted_iota(jnp.int32, (8, 128), 0)
     lane = lax.broadcasted_iota(jnp.int32, (8, 128), 1)
     odd = ((rowi + lane) & 1) == 1
-    first, last = lane == 0, lane == 127
 
     def out_copy(k, slot):
         return pltpu.make_async_copy(outs.at[slot], out_hbm.at[pl.ds(2 * k, 2)], out_sem.at[slot])
@@ -256,35 +307,8 @@
     zero = jnp.zeros((8, 128), F32)
     for j in range(NJ):
         for i in range(ROWS // 8):
-            x = r_0[pl.ds(row(0, j, 8 * i), 8), :]
-            for ref in (r_1, b_1, r_2):
-                ref[pl.ds(row(NK + 1, j, 8 * i), 8), :] = zero
-                ref[pl.ds(row(0, j, 8 * i), 8), :] = x
-
-    def half(k, colour, src, own, rho, nj, emit):
-        st = (k + 1) * PITCH
-        co = (k + colour * NK) * PITCH
-        cen = [src[pl.ds(st + j * ROWS + rho, 8), :] for j in range(NJ)]
-        rl = [pltpu.roll(x, 1, 1) for x in cen]
-        rr = [pltpu.roll(x, 127, 1) for x in cen]
-        for j in range(nj):
-            off = j * ROWS + rho
-            left = jnp.where(first, rl[(j - 1) % NJ], rl[j])
-            right = jnp.where(last, rr[(j + 1) % NJ], rr[j])
-            lo, hi = src[pl.ds(st - PITCH + off, 8), :], src[pl.ds(st + PITCH + off, 8), :]
-            rad = jnp.where(odd, hi, lo) if colour == 0 else jnp.where(odd, lo, hi)
-            d1 = src[pl.ds(st + off + 1, 8), :] - src[pl.ds(st + off - 1, 8), :]
-            d2 = own[pl.ds(st + off + 2, 8), :] - own[pl.ds(st + off - 2, 8), :]
-            acc = ((jg[pl.ds(co + off, 8), :] + rad) + cen[j]) + (left + right)
-            emit(j, rho, acc * 0.25 - sg[pl.ds(co + off, 8), :] * (d1 * 8.0 - d2))
-
-    def unit(k, colour, src, own, dst):
-        st = (k + 1) * PITCH
-
-        def emit(j, rho, val):
-            dst[pl.ds(st + j * ROWS + rho, 8), :] = val
-        for i in range(17):
-            half(k, colour, src, own, 8 + 8 * i, NJ, emit)
+            r_2[pl.ds(row(NK + 1, j, 8 * i), 8), :] = zero
+            r_2[pl.ds(row(0, j, 8 * i), 8), :] = b_0[pl.ds(row(0, j, 8 * i), 8), :]
 
     def final(k, slot):
         st = (k + 1) * PITCH
@@ -295,20 +319,30 @@
             outs[slot, 0, t:t + 8, 128 * j:128 * j + 128] = jnp.where(odd, val, red)
             outs[slot, 1, t:t + 8, 128 * j:128 * j + 128] = jnp.where(odd, red, val)
         for i in range(16):
-            half(k, 1, r_2, b_1, T0 + 8 * i, 8, emit)
+            half(k, 1, r_2, b_1, sg, jg, T0 + 8 * i, 8, emit)
+
+    edge_0, edge_1 = (0, 16), (0, 1, 15, 16)
 
     def step(s, _):
-        @pl.when(s < NK)
-        def _():
-            unit(NK - 1 - s, 0, b_0, r_0, r_1)
-
-        @pl.when((s >= 1) & (s < NK + 1))
-        def _():
-            unit(NK - s, 1, r_1, b_0, b_1)
+        @pl.when(s < NK - 1)
+        def _():
+            update(NK - 1 - s, 0, b_0, r_0, r_1, sg, jg, edge_0)
+
+        @pl.when(s == NK - 1)
+        def _():
+            update(0, 0, b_0, r_0, r_1, sg, jg, range(17))
+
+        @pl.when((s >= 1) & (s < NK - 1))
+        def _():
+            update(NK - s, 1, r_1, b_0, b_1, sg, jg, edge_1)
+
+        @pl.when((s >= NK - 1) & (s < NK + 1))
+        def _():
+            update(NK - s, 1, r_1, b_0, b_1, sg, jg, range(17))
 
         @pl.when((s >= 2) & (s < NK + 2))
         def _():
-            unit(NK + 1 - s, 0, b_1, r_1, r_2)
+            update(NK + 1 - s, 0, b_1, r_1, r_2, sg, jg, range(17))
 
         @pl.when(s >= 3)
         def _():
@@ -335,33 +369,36 @@
     coef = V((2 * NK * PITCH, 128), F32)
     packed = pl.pallas_call(
         exchange,
-        out_shape=(state, state, coef, coef),
+        out_shape=(state, state, coef, coef, state, state),
         in_specs=[anys] * 4 + [vm],
-        out_specs=(vm,) * 4,
+        out_specs=(vm,) * 6,
         scratch_shapes=[V((2, 2, 128, 1024), F32), V((2, 2, 128, 1024), BF16), V((2, 2, 128, 1024), BF16),
                         V((2, 16, 8, 1024), F32), V((2, 16, 8, 1024), BF16), V((2, 16, 8, 1024), BF16),
-                        V((3 * 2 * 8 * 128, 128), F32),
-                        V((2, 9, 8, 1024), F32), V((2, 5, 8, 1024), BF16), V((2, 5, 8, 1024), BF16),
-                        V((2, 9, 8, 1024), F32), V((2, 5, 8, 1024), BF16), V((2, 5, 8, 1024), BF16),
+                        V((2 * 8 * 128, 128), F32),
+                        V((2, 2, 8, 1024), F32), V((2, 17, 8, 1024), BF16),
+                        V((2, 2, 8, 1024), F32), V((2, 17, 8, 1024), BF16),
                         V((2, 16, 128, 128), F32), V((2, 16, 128, 128), BF16), V((2, 16, 128, 128), BF16),
                         V((128, 128), F32), V((128, 128), BF16), V((128, 128), BF16), V((2, 3, 8, 128), F32),
-                        V((2, 128, 128), F32), V((2, 128, 128), BF16), V((2, 128, 128), BF16), V((2, 2, 3, 8, 128), F32),
+                        V((2, 64, 128), F32), V((2, 64, 128), BF16), V((2, 64, 128), BF16),
+                        V((2, 64, 128), F32), V((2, 64, 128), BF16), V((2, 64, 128), BF16), V((2, 2, 3, 8, 128), F32),
                         V((16, 8192), BF16), V((16, 8192), BF16), V((8, 9, 16, 128), BF16),
                         V((9, 128, 128), BF16), V((2, 9, 16, 128), BF16),
                         D((3, 2)), D((3, 2)), D((3, 2)), D((2,)), D((7,)), D((7,)), D((7,)), D((7,)), D((2, 3)), D((2, 3)),
-                        D((2, 3)), D((2, 3)), D((2, 2)), D((2, 2)), D((8,)), D((2,))],
+                        D((2, 2)), D((2, 2)), D((2, 2)), D((2, 2)), D((8,)), D((2,))],
         compiler_params=pltpu.CompilerParams(collective_id=0, has_side_effects=True, vmem_limit_bytes=LIMIT),
         name="exchange",
     )(u, s, c, rot, sk)
-    return pl.pallas_call(
+    out, _, _ = pl.pallas_call(
         relax,
-        out_shape=jax.ShapeDtypeStruct((16, 128, 1024), F32),
-        in_specs=[vm] * 4,
-        out_specs=anys,
-        scratch_shapes=[state, state, state, V((2, 2, 128, 1024), F32), D((2,))],
-        compiler_params=pltpu.CompilerParams(vmem_limit_bytes=LIMIT2),
+        out_shape=(jax.ShapeDtypeStruct((16, 128, 1024), F32), state, state),
+        in_specs=[vm] * 6,
+        out_specs=(anys, vm, vm),
+        scratch_shapes=[state, V((2, 2, 128, 1024), F32), D((2,))],
+        input_output_aliases={4: 1, 5: 2},
+        compiler_params=pltpu.CompilerParams(vmem_limit_bytes=LIMIT),
         name="relax",
     )(*[pltpu.with_memory_space_constraint(x, pltpu.VMEM) for x in packed])
+    return out
 
 
 def solution(mesh):

time: 51.3 us -> 51 us (level)
  no operation moved by 1% of the time
where the time goes in v1:
time: 51 us; the launch traced here: 50.7 us
  Pallas kernels  49.4 us (97%)
  local copies, waits for them, and re-layouts  1.37 us (3%)
    pallas_call x1, Pallas kernels, local(): pl.pallas_call(exchange, out_shape=(state, state, coef, coef, state, stat...  36.3 us
    pallas_call x1, Pallas kernels, local(): pl.pallas_call(relax, out_shape=(jax.ShapeDtypeStruct((16, 128, 1024), F3...  13 us
    broadcast_in_dim x1, local copies, waits for them, and re-layouts, local(): sk = jnp.broadcast_to(skew[:, None], (128, 128))  1.37 us

profile of v1, /device:TPU:0, one launch (start us, length us, event | category | flops | bytes accessed | tf_op | source)
XLA Modules:
  0.0 50.7 jit_solution(14933633739395508183)
XLA Ops:
  0.0 1.4 %broadcast_in_dim.2.sk = s32[128,128]{1,0:T(8,128)} broadcast(s32[128]{0:T(128)} %param.9), dimensions={0} | broadcast | bytes 66048 | tf_op jit(solution)/shard_map/broadcast_in_dim | solution.py:364
  1.4 36.3 %exchange.1 = (f32[13680,128]{1,0:T(8,128)S(1)}, f32[13680,128]{1,0:T(8,128)S(1)}, f32[21888,128]{1,0:T(8,128)S(1)}, f32[21888,128]{1,0:T(8,128)S(1)}, f32[13680...) custom-call(f32[16,128,1024]{2,1,0:T(8,128)} %u_hbm.1, bf16[16,128,1024]{2,1,0:T(8,128)(2,1)} %s_hbm.1, ...), custom_call_target="tpu_custom_call" | custom-call | tf_op jit(solution)/shard_map/exchange/pallas_call | solution.py:370
  37.7 13.0 %relax.1 = (f32[16,128,1024]{2,1,0:T(8,128)}, f32[13680,128]{1,0:T(8,128)S(1)}, f32[13680,128]{1,0:T(8,128)S(1)}) custom-call(f32[13680,128]{1,0:T(8,128)S(1)} %get-tuple-element.12.r_0, f32[13680,128]{1,0:T(8,128)S(1)} %get-tuple-element.13.b_0, f32[21888,128]{1,0:T(8,128)S(1)} %get-tuple-element.14.sg, ...), custom_call_target="tpu_custom_call", output_to_operand_aliasing={{1}: (4, {}), {2}: (5, {})} | custom-call | tf_op jit(solution)/shard_map/relax/pallas_call | solution.py:391

commit v2 on v1

--- a/solution.py
+++ b/solution.py
@@ -97,8 +97,8 @@
     for t in (up, down):
         for a in range(NAZ):
             pl.semaphore_signal(barrier, inc=1, device_id={"ta": t, "az": a}, device_id_type=MESH)
+    for c in cols: c.start()
     for c in edges: c.start()
-    for c in cols: c.start()
     own = pltpu.make_async_copy(rot_hbm.at[pl.ds(16 * az, 16), :], w0.at[:, pl.ds(1024 * az, 1024)], own_sem.at[0])
     own.start()
     for c in in_copies(NK - 1, 0): c.start()
@@ -107,32 +107,6 @@
     first_hop = [remote(rot_hbm.at[pl.ds(16 * d, 16), :], w0.at[:, pl.ds(1024 * az, 1024)], p1s.at[o], p1r.at[o], {"az": d})
                  for o, d in enumerate(others)]
     for c in first_hop: c.start()
-
-    for c in edges: c.wait()
-    for side in range(2):
-        for q, e in enumerate((eu, es, ec)):
-            for j in range(8):
-                ln = slice(128 * j, 128 * j + 128)
-                base = (side * 8 + j) * 128
-                for k in range(NK):
-                    even, odd_layer = e[side, 2 * k, :, ln].astype(F32), e[side, 2 * k + 1, :, ln].astype(F32)
-                    er[base + 8 * k:base + 8 * k + 8, :] = jnp.where(odd, odd_layer, even)
-                    er[base + 64 + 8 * k:base + 72 + 8 * k, :] = jnp.where(odd, even, odd_layer)
-                if q == 0:
-                    for i, t in enumerate(RED_ROWS[side]):
-                        tb[side, i, :, ln] = er[pl.ds(base + t, NK, stride=8), :].astype(BF16)
-                    for i, t in enumerate(BLACK_ROWS[side]):
-                        tile = er[pl.ds(base + 64 + t, NK, stride=8), :]
-                        if i < 2:
-                            su[side, i, :, ln] = tile
-                        else:
-                            tb[side, 3 + i, :, ln] = tile.astype(BF16)
-                else:
-                    for i, (t, colour) in enumerate(COEF_ROWS[side]):
-                        tb[side, 2 + 5 * q + i, :, ln] = er[pl.ds(base + 64 * colour + t, NK, stride=8), :].astype(BF16)
-    time_hop = [remote(a.at[side], b.at[side], tas.at[side, q], tar.at[side, q], {"ta": d})
-                for side, d in ((0, down), (1, up)) for q, (a, b) in enumerate(((su, hu), (tb, hb)))]
-    for c in time_hop: c.start()
 
     for c in cols: c.wait()
 
@@ -164,6 +138,32 @@
                 for side, other, t, a in diagonals]
     for c in az_hop + diag_hop: c.start()
 
+    for c in edges: c.wait()
+    for side in range(2):
+        for q, e in enumerate((eu, es, ec)):
+            for j in range(8):
+                ln = slice(128 * j, 128 * j + 128)
+                base = (side * 8 + j) * 128
+                for k in range(NK):
+                    even, odd_layer = e[side, 2 * k, :, ln].astype(F32), e[side, 2 * k + 1, :, ln].astype(F32)
+                    er[base + 8 * k:base + 8 * k + 8, :] = jnp.where(odd, odd_layer, even)
+                    er[base + 64 + 8 * k:base + 72 + 8 * k, :] = jnp.where(odd, even, odd_layer)
+                if q == 0:
+                    for i, t in enumerate(RED_ROWS[side]):
+                        tb[side, i, :, ln] = er[pl.ds(base + t, NK, stride=8), :].astype(BF16)
+                    for i, t in enumerate(BLACK_ROWS[side]):
+                        tile = er[pl.ds(base + 64 + t, NK, stride=8), :]
+                        if i < 2:
+                            su[side, i, :, ln] = tile
+                        else:
+                            tb[side, 3 + i, :, ln] = tile.astype(BF16)
+                else:
+                    for i, (t, colour) in enumerate(COEF_ROWS[side]):
+                        tb[side, 2 + 5 * q + i, :, ln] = er[pl.ds(base + 64 * colour + t, NK, stride=8), :].astype(BF16)
+    time_hop = [remote(a.at[side], b.at[side], tas.at[side, q], tar.at[side, q], {"ta": d})
+                for side, d in ((0, down), (1, up)) for q, (a, b) in enumerate(((su, hu), (tb, hb)))]
+    for c in time_hop: c.start()
+
     def pack(s, _):
         k = NK - 1 - s
         slot = lax.rem(s, 2)
@@ -190,7 +190,8 @@
 
     own.wait()
     for c in first_hop: c.wait_recv()
-    amount = sk[pl.ds(pl.multiple_of(16 * az, 16), 16), :]
+    here = jnp.where(lane16 == row16 + 16 * az, jnp.broadcast_to(sk[...], (16, 128)).astype(F32), 0.0)
+    amount = jnp.broadcast_to(jnp.sum(here, axis=1, keepdims=True).astype(jnp.int32), (16, 128))
     src, dst = w0, w1
     for b in range(6):
         bit = ((amount >> b) & 1) == 1
@@ -361,7 +362,7 @@
 
 
 def local(u, s, c, rot, skew):
-    sk = jnp.broadcast_to(skew[:, None], (128, 128))
+    sk = skew.reshape(1, 128)
     anys = pl.BlockSpec(memory_space=pl.ANY)
     vm = pl.BlockSpec(memory_space=pltpu.VMEM)
     D, V = pltpu.SemaphoreType.DMA, pltpu.VMEM

time: 51 us -> 48.8 us (0.957)
  the two profiles are of different devices: /device:TPU:0 before, /device:TPU:39 now
where the time goes in v2:
time: 48.8 us; the launch traced here: 48.6 us
  Pallas kernels  48.6 us (100%)
    pallas_call x1, Pallas kernels, local(): pl.pallas_call(exchange, out_shape=(state, state, coef, coef, state, stat...  35.5 us
    pallas_call x1, Pallas kernels, local(): pl.pallas_call(relax, out_shape=(jax.ShapeDtypeStruct((16, 128, 1024), F3...  13 us

profile of v2, /device:TPU:39, one launch (start us, length us, event | category | flops | bytes accessed | tf_op | source)
XLA Modules:
  0.0 48.6 jit_solution(4904698806690768524)
XLA Ops:
  0.0 35.5 %exchange.1 = (f32[13680,128]{1,0:T(8,128)S(1)}, f32[13680,128]{1,0:T(8,128)S(1)}, f32[21888,128]{1,0:T(8,128)S(1)}, f32[21888,128]{1,0:T(8,128)S(1)}, f32[13680...) custom-call(f32[16,128,1024]{2,1,0:T(8,128)} %u_hbm.1, bf16[16,128,1024]{2,1,0:T(8,128)(2,1)} %s_hbm.1, ...), custom_call_target="tpu_custom_call" | custom-call | tf_op jit(solution)/shard_map/exchange/pallas_call | solution.py:371
  35.5 13.0 %relax.1 = (f32[16,128,1024]{2,1,0:T(8,128)}, f32[13680,128]{1,0:T(8,128)S(1)}, f32[13680,128]{1,0:T(8,128)S(1)}) custom-call(f32[13680,128]{1,0:T(8,128)S(1)} %get-tuple-element.12.r_0, f32[13680,128]{1,0:T(8,128)S(1)} %get-tuple-element.13.b_0, f32[21888,128]{1,0:T(8,128)S(1)} %get-tuple-element.14.sg, ...), custom_call_target="tpu_custom_call", output_to_operand_aliasing={{1}: (4, {}), {2}: (5, {})} | custom-call | tf_op jit(solution)/shard_map/relax/pallas_call | solution.py:392

commit v3 on v2

--- a/solution.py
+++ b/solution.py
@@ -212,6 +212,8 @@
     beyond = [[remote(v.at[d], cych.at[side], cys.at[d], cyr.at[side], {"ta": t, "az": d}) for d in range(NAZ)]
               for side, t in ((0, down), (1, up))]
 
+    lax.fori_loop(0, NK, pack, 0)
+
     @pl.when(az == NAZ - 1)
     def _():
         for c in beyond[0]: c.start()
@@ -219,8 +221,6 @@
     @pl.when(az == 0)
     def _():
         for c in beyond[1]: c.start()
-
-    lax.fori_loop(0, NK, pack, 0)
 
     zero = jnp.zeros((8, 128), F32)
     for j in range(NJ):

time: 48.8 us -> 48.4 us (level)
  no operation moved by 1% of the time
where the time goes in v3:
time: 48.4 us; the launch traced here: 48.2 us
  Pallas kernels  48.2 us (100%)
    pallas_call x1, Pallas kernels, local(): pl.pallas_call(exchange, out_shape=(state, state, coef, coef, state, stat...  35.1 us
    pallas_call x1, Pallas kernels, local(): pl.pallas_call(relax, out_shape=(jax.ShapeDtypeStruct((16, 128, 1024), F3...  13 us

profile of v3, /device:TPU:39, one launch (start us, length us, event | category | flops | bytes accessed | tf_op | source)
XLA Modules:
  0.0 48.2 jit_solution(5156444008559345953)
XLA Ops:
  0.0 35.1 %exchange.1 = (f32[13680,128]{1,0:T(8,128)S(1)}, f32[13680,128]{1,0:T(8,128)S(1)}, f32[21888,128]{1,0:T(8,128)S(1)}, f32[21888,128]{1,0:T(8,128)S(1)}, f32[13680...) custom-call(f32[16,128,1024]{2,1,0:T(8,128)} %u_hbm.1, bf16[16,128,1024]{2,1,0:T(8,128)(2,1)} %s_hbm.1, ...), custom_call_target="tpu_custom_call" | custom-call | tf_op jit(solution)/shard_map/exchange/pallas_call | solution.py:371
  35.1 13.0 %relax.1 = (f32[16,128,1024]{2,1,0:T(8,128)}, f32[13680,128]{1,0:T(8,128)S(1)}, f32[13680,128]{1,0:T(8,128)S(1)}) custom-call(f32[13680,128]{1,0:T(8,128)S(1)} %get-tuple-element.12.r_0, f32[13680,128]{1,0:T(8,128)S(1)} %get-tuple-element.13.b_0, f32[21888,128]{1,0:T(8,128)S(1)} %get-tuple-element.14.sg, ...), custom_call_target="tpu_custom_call", output_to_operand_aliasing={{1}: (4, {}), {2}: (5, {})} | custom-call | tf_op jit(solution)/shard_map/relax/pallas_call | solution.py:392
